TPU v7x, 128 devices: a whole 4x4x4 slice. The times are simulated.
128 devices in a mesh: grid: 8 (over y, core), dom: 16 (over x, z).
Axes of the slice: x: 4, y: 4, z: 4, core: 2. Of those that a mesh axis runs over, the one named last changes fastest.
Arguments:
- home: int32 [1024], P(('grid', 'dom')), may hold values from 0 to 1023, as said below
- p_grid: bfloat16 [1024, 5, 128, 128], P(('grid', 'dom')), may hold values from -0.25 to 0.25
- p_mask: int32 [1024, 5], P(('grid', 'dom')), may hold values 0 or 1
- h_grid: bfloat16 [1024, 5, 128, 128], P(('grid', 'dom')), may hold values from -0.25 to 0.25
- h_mask: int32 [1024, 5], P(('grid', 'dom')), may hold values 0 or 1
- x_inv: bfloat16 [1024, 5, 128, 128], P(('grid', 'dom')), may hold values from -1.1953125 to 1.1953125
- x_mask: int32 [1024, 5], P(('grid', 'dom')), may hold values 0 or 1
Outputs:
- density: bfloat16 [1024, 5, 128, 128], P(('grid', 'dom'))
- energy_density: bfloat16 [1024, 5, 128, 128], P(('grid', 'dom'))
Inputs may be any that keep to these rules, and one draw needn't show every extreme that they name: home is a permutation of the block rows; each block row stays in its domain of 16 devices (128 rows), and one device of the grid layout sends at most ceil(8 / 16) rows to any one device of the domain layout, a count that is reached.
All inputs are finite; a program needn't handle non-finite values. No bound on the sum of `p_mask` or of `h_mask` or of `x_mask` on one device may be relied on, other than what follows from the above.
Results may differ from a plain program's by a relative error of at most 0.0065.
Values may be sent and summed in bfloat16 or wider, within the bound.
A program may use at most 128 MiB of HBM per device.

v0:
```python
import jax
import jax.numpy as jnp
from jax import lax
from jax.sharding import PartitionSpec as P


def with_halo(x, sides, width):
    for axis, dim in sides:
        size, length = (lax.axis_size(axis), x.shape[dim])
        up = [(i, (i + 1) % size) for i in range(size - 1)]
        down = [(j, i) for i, j in up]
        last = lax.slice_in_dim(x, length - width, length, axis=dim)
        leading = lax.slice_in_dim(x, 0, width, axis=dim)
        before = lax.ppermute(last, axis, up)
        after = lax.ppermute(leading, axis, down)
        x = jnp.concatenate([before, x, after], axis=dim)
    return x


def band_product(left, right, left_half, right_half, out_half, offset):
    count = left.shape[0]
    pieces = []
    for o in range(-out_half, out_half + 1):
        total = jnp.zeros((count, left.shape[2], right.shape[3]), jnp.float32)
        for a in range(-left_half, left_half + 1):
            b = o - a
            if -right_half <= b <= right_half:
                rows_b = right[offset + a : offset + a + count, b + right_half]
                total = total + jnp.einsum(
                    "nxy,nyz->nxz",
                    left[:, a + left_half],
                    rows_b,
                    preferred_element_type=jnp.float32,
                )
        pieces.append(total)
    return jnp.stack(pieces, 1)


def shards(home, p_grid, p_mask, h_grid, h_mask, x_inv, x_mask):
    rows = home.shape[0]
    group = lax.axis_size("dom")
    slots_per = (rows + group - 1) // group
    total_slots = group * slots_per
    target_dev = home // rows % group
    target_row = home % rows
    row_ids = jnp.arange(rows, dtype=jnp.int32)
    earlier = (target_dev[:, None] == target_dev[None, :]) & (row_ids[None, :] < row_ids[:, None])
    rank = jnp.sum(earlier.astype(jnp.int32), 1)
    slot_id = target_dev * slots_per + rank
    slot_ids = jnp.arange(total_slots, dtype=jnp.int32)
    match = (slot_id[None, :] == slot_ids[:, None]).astype(jnp.int32)
    source = jnp.sum(match * row_ids[None, :], 1)
    valid = jnp.sum(match, 1)
    keep = valid.astype(jnp.bfloat16)[:, None, None, None]
    p_send = (p_grid * p_mask[:, :, None, None].astype(jnp.bfloat16))[source] * keep
    h_send = (h_grid * h_mask[:, :, None, None].astype(jnp.bfloat16))[source] * keep
    row_send = jnp.where(valid > 0, target_row[source], -1)
    p_recv, h_recv, row_recv = (
        lax.all_to_all(p_send, "dom", split_axis=0, concat_axis=0, tiled=True),
        lax.all_to_all(h_send, "dom", split_axis=0, concat_axis=0, tiled=True),
        lax.all_to_all(row_send, "dom", split_axis=0, concat_axis=0, tiled=True),
    )
    place = (row_recv[None, :] == row_ids[:, None]).astype(jnp.int32)
    picked = jnp.sum(place * slot_ids[None, :], 1)
    p_dom = p_recv[picked]
    h_dom = h_recv[picked]
    x_dom = x_inv * x_mask[:, :, None, None].astype(jnp.bfloat16)
    h_wide = with_halo(h_dom, ((("grid", "dom"), 0),), 4)
    x_wide = with_halo(x_dom, ((("grid", "dom"), 0),), 8)
    p_wide = with_halo(p_dom, ((("grid", "dom"), 0),), 6)
    left_product = band_product(x_wide[8 : 8 + rows], p_wide, 2, 2, 4, 6).astype(jnp.bfloat16)
    right_wide = band_product(p_wide, x_wide, 2, 2, 4, 2).astype(jnp.bfloat16)
    density = band_product(left_product, x_wide, 4, 2, 2, 8).astype(jnp.bfloat16)
    weighted = band_product(left_product, h_wide, 4, 2, 6, 4).astype(jnp.bfloat16)
    energy_density = band_product(weighted, right_wide, 6, 4, 2, 6).astype(jnp.bfloat16)
    return (density, energy_density)


def solution(mesh):
    return jax.shard_map(
        shards,
        mesh=mesh,
        in_specs=(
            P(("grid", "dom")),
            P(("grid", "dom"), None, None, None),
            P(("grid", "dom"), None),
            P(("grid", "dom"), None, None, None),
            P(("grid", "dom"), None),
            P(("grid", "dom"), None, None, None),
            P(("grid", "dom"), None),
        ),
        out_specs=(P(("grid", "dom"), None, None, None), P(("grid", "dom"), None, None, None)),
        check_vma=False,
    )
```

profile of v0, /device:TPU:119, one launch (start us, length us, event | category | flops | bytes accessed | tf_op | source)
XLA Modules:
  0.0 310.3 jit_solution(4657749783896565299)
XLA Ops:
  3.0 6.3 %all-to-all-start.1 = ((s32[16,1,1]{2,1,0:T(1,128)}), s32[16,1,1]{2,1,0:T(1,128)S(1)}, u32[]{:S(2)}, u32[]{:S(2)}) async-start(s32[16,1,1]{2,1,0:T(1,128)} %copy.86), calls=%async_computation.1 | async-start | bytes 16384 | tf_op jit(solution)/shard_map/all_to_all | solution.py:61
  10.0 1.5 broadcast_multiply_fusion.2
  11.5 2.4 gather_fusion.3
  14.0 2.3 gather_fusion
  16.4 4.4 %broadcast_multiply_fusion = (bf16[16,5,128,128]{3,2,1,0:T(8,128)(2,1)S(1)}, bf16[16,5,128,128]{3,2,1,0:T(8,128)(2,1)}) fusion(bf16[16,5,128,128]{3,2,1,0:T(8,128)(2,1)} %gather_fusion.3, bf16[16]{0:T(256)(128)(2,1)S(1)} %get-tuple-element.30, bf16[16,5,128,128]{3,2,1,0:T(8,128)(2,1)} %gather_fusion), kind=kLoop, calls=%fused_computation.68 | loop fusion | flops 2621440 | bytes 10485792 | tf_op jit(solution)/shard_map/mul | solution.py:56
  20.8 34.7 %all_to_all.16 = bf16[16,5,128,128]{3,2,1,0:T(8,128)(2,1)} all-to-all(bf16[16,5,128,128]{3,2,1,0:T(8,128)(2,1)S(1)} %get-tuple-element.27), channel_id=1, replica_groups=mesh['grid'=8,'dom'=16] {'dom'}, dimensions={0} | all-to-all | bytes 5242880 | tf_op jit(solution)/shard_map/all_to_all | solution.py:60
  55.5 8.3 %all-to-all-start = ((bf16[16,5,128,128]{3,2,1,0:T(8,128)(2,1)}), bf16[16,5,128,128]{3,2,1,0:T(8,128)(2,1)}, u32[]{:S(2)}, u32[]{:S(2)}) async-start(bf16[16,5,128,128]{3,2,1,0:T(8,128)(2,1)} %get-tuple-element.28), calls=%async_computation | async-start | bytes 5242880 | tf_op jit(solution)/shard_map/all_to_all | solution.py:59
  64.0 5.8 %collective-permute-start.1 = (bf16[8,5,128,128]{3,2,0,1:T(8,128)(2,1)S(1)}, bf16[8,5,128,128]{3,2,0,1:T(8,128)(2,1)}, u32[]{:S(2)}, u32[]{:S(2)}) collective-permute-start(bf16[8,5,128,128]{3,2,0,1:T(8,128)(2,1)S(1)} %copy_multiply_fusion), channel_id=1, source_target_pairs={{0,1},{1,2},{2,3},{3,4},{4,5},{5,6},{6,7},{7,8},{8,9},{9,10},{10,1... | collective-permute-start | bytes 3932168 | tf_op jit(solution)/shard_map/ppermute | solution.py:14
  69.8 1.9 collective-permute-start.3
  72.3 49.9 %collective-permute-done.1 = bf16[8,5,128,128]{3,2,0,1:T(8,128)(2,1)} collective-permute-done((bf16[8,5,128,128]{3,2,0,1:T(8,128)(2,1)S(1)}, bf16[8,5,128,128]{3,2,0,1:T(8,128)(2,1)}, u32[]{:S(2)}, u32[]{:S(2)}) %collective-permute-start.1) | collective-permute-done | bytes 1310752 | tf_op jit(solution)/shard_map/ppermute | solution.py:14
  122.1 2.4 collective-permute-done.3
  124.5 3.2 %pad_maximum_fusion = bf16[24,5,128,128]{3,2,0,1:T(8,128)(2,1)} fusion(bf16[8,5,128,128]{3,2,0,1:T(8,128)(2,1)S(1)} %collective-permute-done.3, bf16[8,5,128,128]{3,2,0,1:T(8,128)(2,1)S(1)} %copy_multiply_fusion, bf16[8,5,128,128]{3,2,0,1:T(8,128)(2,1)} %collective-permute-done.1), kind=kLoop, calls=%fused_computation.41 | loop fusion | flops 3932160 | bytes 7864320 | tf_op jit(solution)/shard_map/concatenate | solution.py:16
  127.8 3.5 %gather_fusion.4 = bf16[8,5,128,128]{3,2,1,0:T(8,128)(2,1)} fusion(bf16[16,5,128,128]{3,2,1,0:T(8,128)(2,1)} %all_to_all.16, s32[1024]{0:T(1024)S(1)} %pad_clamp_fusion), kind=kCustom, calls=%fused_computation.4 | custom fusion | bytes 2621472 | tf_op jit(solution)/shard_map/gather | solution.py:66
  131.3 2.2 fusion.282
  133.6 4.7 %collective-permute-start.4 = (bf16[4,5,128,128]{3,2,0,1:T(8,128)(2,1)}, bf16[4,5,128,128]{3,2,0,1:T(8,128)(2,1)}, u32[]{:S(2)}, u32[]{:S(2)}) collective-permute-start(bf16[4,5,128,128]{3,2,0,1:T(8,128)(2,1)} %get-tuple-element.15), channel_id=1, source_target_pairs={{0,1},{1,2},{2,3},{3,4},{4,5},{5,6},{6,7},{7,8},{8,9},{9,10},{10,1... | collective-permute-start | bytes 1966088 | tf_op jit(solution)/shard_map/ppermute | solution.py:14
  138.2 3.5 %gather_fusion.2 = bf16[8,5,128,128]{3,2,1,0:T(8,128)(2,1)} fusion(bf16[16,5,128,128]{3,2,1,0:T(8,128)(2,1)} %all-to-all-done, s32[1024]{0:T(1024)S(1)} %pad_clamp_fusion), kind=kCustom, calls=%fused_computation.2 | custom fusion | bytes 2621472 | tf_op jit(solution)/shard_map/gather | solution.py:65
  141.8 1.7 fusion.283
  143.5 1.9 collective-permute-start
  145.4 3.4 %collective-permute-start.2 = (bf16[6,5,128,128]{3,2,0,1:T(8,128)(2,1)S(1)}, bf16[6,5,128,128]{3,2,0,1:T(8,128)(2,1)S(1)}, u32[]{:S(2)}, u32[]{:S(2)}) collective-permute-start(bf16[6,5,128,128]{3,2,0,1:T(8,128)(2,1)S(1)} %get-tuple-element.22), channel_id=1, source_target_pairs={{1,0},{2,1},{3,2},{4,3},{5,4},{6,5},{7,6},{8,7},{9,8},{10,9},{11,1... | collective-permute-start | bytes 2949128 | tf_op jit(solution)/shard_map/ppermute | solution.py:15
  148.8 2.1 collective-permute-start.5
  151.4 1.7 collective-permute-done.4
  154.9 33.6 %collective-permute-done.5 = bf16[4,5,128,128]{3,2,0,1:T(8,128)(2,1)S(1)} collective-permute-done((bf16[4,5,128,128]{3,2,0,1:T(8,128)(2,1)S(1)}, bf16[4,5,128,128]{3,2,0,1:T(8,128)(2,1)S(1)}, u32[]{:S(2)}, u32[]{:S(2)}) %collective-permute-start.5) | collective-permute-done | bytes 655392 | tf_op jit(solution)/shard_map/ppermute | solution.py:15
  194.8 1.3 copy-done
  196.0 1.2 convolution_convert_fusion.1
  197.2 1.4 fusion.102
  200.9 1.4 fusion.100
  202.3 1.4 fusion.101
  204.8 1.4 fusion.97
  206.2 1.4 fusion.98
  207.6 1.4 fusion.99
  210.0 1.4 fusion.93
  211.4 1.4 fusion.94
  212.8 1.4 fusion.95
  214.2 1.4 fusion.96
  215.6 1.4 fusion.90
  217.0 1.4 fusion.91
  218.4 1.4 fusion.92
  219.8 1.5 fusion.88
  221.3 1.4 fusion.89
  226.3 1.4 fusion.87
  231.1 1.1 convolution_convert_fusion
  232.3 1.2 fusion.168
  258.6 2.1 fusion.78
  260.7 1.4 fusion.55
  262.2 1.7 fusion.9
  271.5 1.4 copy-done.1
  305.2 2.1 fusion.67
  307.3 2.5 copy.107
  (298 shorter events, 87.9 us)
Async XLA Ops:
  3.0 17.9 %all-to-all-start.1 = ((s32[16,1,1]{2,1,0:T(1,128)}), s32[16,1,1]{2,1,0:T(1,128)S(1)}, u32[]{:S(2)}, u32[]{:S(2)}) async-start(s32[16,1,1]{2,1,0:T(1,128)} %copy.86), calls=%async_computation.1 | async-start | bytes 16384 | tf_op jit(solution)/shard_map/all_to_all | solution.py:61
  11.5 2.4 copy-start.63
  11.5 2.4 copy-start.61
  55.5 8.3 %copy-start.64 = (s32[8,5]{1,0:T(8,128)S(1)}, s32[8,5]{1,0:T(8,128)}, u32[]{:S(2)}) copy-start(s32[8,5]{1,0:T(8,128)} %param.13) | copy-start | bytes 484
  55.5 8.4 %copy-start.62 = (bf16[8,5,128,128]{3,2,1,0:T(8,128)(2,1)S(1)}, bf16[8,5,128,128]{3,2,1,0:T(8,128)(2,1)}, u32[]{:S(2)}) copy-start(bf16[8,5,128,128]{3,2,1,0:T(8,128)(2,1)} %param.12) | copy-start | bytes 3932164
  55.5 82.7 %all-to-all-start = ((bf16[16,5,128,128]{3,2,1,0:T(8,128)(2,1)}), bf16[16,5,128,128]{3,2,1,0:T(8,128)(2,1)}, u32[]{:S(2)}, u32[]{:S(2)}) async-start(bf16[16,5,128,128]{3,2,1,0:T(8,128)(2,1)} %get-tuple-element.28), calls=%async_computation | async-start | bytes 5242880 | tf_op jit(solution)/shard_map/all_to_all | solution.py:59
  64.0 58.1 %collective-permute-start.1 = (bf16[8,5,128,128]{3,2,0,1:T(8,128)(2,1)S(1)}, bf16[8,5,128,128]{3,2,0,1:T(8,128)(2,1)}, u32[]{:S(2)}, u32[]{:S(2)}) collective-permute-start(bf16[8,5,128,128]{3,2,0,1:T(8,128)(2,1)S(1)} %copy_multiply_fusion), channel_id=1, source_target_pairs={{0,1},{1,2},{2,3},{3,4},{4,5},{5,6},{6,7},{7,8},{8,9},{9,10},{10,1... | collective-permute-start | bytes 3932168 | tf_op jit(solution)/shard_map/ppermute | solution.py:14
  69.8 54.7 %collective-permute-start.3 = (bf16[8,5,128,128]{3,2,0,1:T(8,128)(2,1)S(1)}, bf16[8,5,128,128]{3,2,0,1:T(8,128)(2,1)S(1)}, u32[]{:S(2)}, u32[]{:S(2)}) collective-permute-start(bf16[8,5,128,128]{3,2,0,1:T(8,128)(2,1)S(1)} %copy_multiply_fusion), channel_id=1, source_target_pairs={{1,0},{2,1},{3,2},{4,3},{5,4},{6,5},{7,6},{8,7},{9,8},{10,9},{11,1... | collective-permute-start | bytes 3932168 | tf_op jit(solution)/shard_map/ppermute | solution.py:15
  133.6 19.5 %collective-permute-start.4 = (bf16[4,5,128,128]{3,2,0,1:T(8,128)(2,1)}, bf16[4,5,128,128]{3,2,0,1:T(8,128)(2,1)}, u32[]{:S(2)}, u32[]{:S(2)}) collective-permute-start(bf16[4,5,128,128]{3,2,0,1:T(8,128)(2,1)} %get-tuple-element.15), channel_id=1, source_target_pairs={{0,1},{1,2},{2,3},{3,4},{4,5},{5,6},{6,7},{7,8},{8,9},{9,10},{10,1... | collective-permute-start | bytes 1966088 | tf_op jit(solution)/shard_map/ppermute | solution.py:14
  141.8 9.1 %copy-start.4 = (bf16[8,5,128,128]{3,2,1,0:T(8,128)(2,1)S(1)}, bf16[8,5,128,128]{3,2,1,0:T(8,128)(2,1)}, u32[]{:S(2)}) copy-start(bf16[8,5,128,128]{3,2,1,0:T(8,128)(2,1)} %gather_fusion.2) | copy-start | bytes 3932164
  143.5 45.1 %collective-permute-start = (bf16[6,5,128,128]{3,2,0,1:T(8,128)(2,1)S(1)}, bf16[6,5,128,128]{3,2,0,1:T(8,128)(2,1)S(1)}, u32[]{:S(2)}, u32[]{:S(2)}) collective-permute-start(bf16[6,5,128,128]{3,2,0,1:T(8,128)(2,1)S(1)} %get-tuple-element.21), channel_id=1, source_target_pairs={{0,1},{1,2},{2,3},{3,4},{4,5},{5,6},{6,7},{7,8},{8,9},{9,10},{10,1... | collective-permute-start | bytes 2949128 | tf_op jit(solution)/shard_map/ppermute | solution.py:14
  145.4 45.9 %collective-permute-start.2 = (bf16[6,5,128,128]{3,2,0,1:T(8,128)(2,1)S(1)}, bf16[6,5,128,128]{3,2,0,1:T(8,128)(2,1)S(1)}, u32[]{:S(2)}, u32[]{:S(2)}) collective-permute-start(bf16[6,5,128,128]{3,2,0,1:T(8,128)(2,1)S(1)} %get-tuple-element.22), channel_id=1, source_target_pairs={{1,0},{2,1},{3,2},{4,3},{5,4},{6,5},{7,6},{8,7},{9,8},{10,9},{11,1... | collective-permute-start | bytes 2949128 | tf_op jit(solution)/shard_map/ppermute | solution.py:15
  148.8 39.7 %collective-permute-start.5 = (bf16[4,5,128,128]{3,2,0,1:T(8,128)(2,1)S(1)}, bf16[4,5,128,128]{3,2,0,1:T(8,128)(2,1)S(1)}, u32[]{:S(2)}, u32[]{:S(2)}) collective-permute-start(bf16[4,5,128,128]{3,2,0,1:T(8,128)(2,1)S(1)} %get-tuple-element.14), channel_id=1, source_target_pairs={{1,0},{2,1},{3,2},{4,3},{5,4},{6,5},{7,6},{8,7},{9,8},{10,9},{11,1... | collective-permute-start | bytes 1966088 | tf_op jit(solution)/shard_map/ppermute | solution.py:15
  151.1 3.0 copy-start.11
  154.9 87.4 %copy-start.13 = (bf16[12,5,128,128]{3,2,0,1:T(8,128)(2,1)}, bf16[12,5,128,128]{3,2,0,1:T(8,128)(2,1)S(1)}, u32[]{:S(2)}) copy-start(bf16[12,5,128,128]{3,2,0,1:T(8,128)(2,1)S(1)} %get-tuple-element.17) | copy-start | bytes 5898244
  188.6 50.1 %copy-start.5 = (bf16[12,5,128,128]{3,2,0,1:T(8,128)(2,1)}, bf16[12,5,128,128]{3,2,0,1:T(8,128)(2,1)S(1)}, u32[]{:S(2)}) copy-start(bf16[12,5,128,128]{3,2,0,1:T(8,128)(2,1)S(1)} %constant_dynamic-update-slice_fusion.9) | copy-start | bytes 5898244
  190.6 61.9 %copy-start.20 = (bf16[8,128,128]{2,1,0:T(8,128)(2,1)}, bf16[8,128,128]{2,1,0:T(8,128)(2,1)S(1)}, u32[]{:S(2)}) copy-start(bf16[8,128,128]{2,1,0:T(8,128)(2,1)S(1)} %convolution_convert_fusion.5) | copy-start | bytes 786436
  191.9 39.2 %copy-start.2 = (bf16[20,5,128,128]{3,2,0,1:T(8,128)(2,1)}, bf16[20,5,128,128]{3,2,0,1:T(8,128)(2,1)S(1)}, u32[]{:S(2)}) copy-start(bf16[20,5,128,128]{3,2,0,1:T(8,128)(2,1)S(1)} %get-tuple-element.23) | copy-start | bytes 9830404
  193.8 2.2 copy-start
  194.5 55.9 %copy-start.22 = (bf16[8,128,128]{2,1,0:T(8,128)(2,1)}, bf16[8,128,128]{2,1,0:T(8,128)(2,1)S(1)}, u32[]{:S(2)}) copy-start(bf16[8,128,128]{2,1,0:T(8,128)(2,1)S(1)} %convolution_convert_fusion.4) | copy-start | bytes 786436
  198.9 52.5 %copy-start.16 = (bf16[8,128,128]{2,1,0:T(8,128)(2,1)}, bf16[8,128,128]{2,1,0:T(8,128)(2,1)S(1)}, u32[]{:S(2)}) copy-start(bf16[8,128,128]{2,1,0:T(8,128)(2,1)S(1)} %fusion.49) | copy-start | bytes 786436
  223.2 33.1 %copy-start.7 = (bf16[8,128,128]{2,1,0:T(8,128)(2,1)}, bf16[8,128,128]{2,1,0:T(8,128)(2,1)S(1)}, u32[]{:S(2)}) copy-start(bf16[8,128,128]{2,1,0:T(8,128)(2,1)S(1)} %fusion.53) | copy-start | bytes 786436
  228.0 22.7 %copy-start.18 = (bf16[8,128,128]{2,1,0:T(8,128)(2,1)}, bf16[8,128,128]{2,1,0:T(8,128)(2,1)S(1)}, u32[]{:S(2)}) copy-start(bf16[8,128,128]{2,1,0:T(8,128)(2,1)S(1)} %fusion.54) | copy-start | bytes 786436
  240.9 13.0 %copy-start.9 = (bf16[8,128,128]{2,1,0:T(8,128)(2,1)}, bf16[8,128,128]{2,1,0:T(8,128)(2,1)S(1)}, u32[]{:S(2)}) copy-start(bf16[8,128,128]{2,1,0:T(8,128)(2,1)S(1)} %fusion.50) | copy-start | bytes 786436
  256.6 2.0 copy-start.14
  256.6 2.0 copy-start.21
  260.7 1.5 copy-start.31
  262.2 1.7 copy-start.49
  266.3 1.8 copy-start.51
  266.6 3.8 %copy-start.50 = (f32[8,128,128]{2,1,0:T(8,128)S(1)}, f32[8,128,128]{2,1,0:T(8,128)}, u32[]{:S(2)}) copy-start(f32[8,128,128]{2,1,0:T(8,128)} %fusion.177) | copy-start | bytes 1572868
  266.8 1.8 copy-start.15
  266.8 1.8 copy-start.17
  266.8 4.0 %copy-start.45 = (f32[8,128,128]{2,1,0:T(8,128)S(1)}, f32[8,128,128]{2,1,0:T(8,128)}, u32[]{:S(2)}) copy-start(f32[8,128,128]{2,1,0:T(8,128)} %fusion.174) | copy-start | bytes 1572868
  268.6 1.5 copy-start.6
  268.8 2.3 copy-start.30
  269.1 2.4 copy-start.3
  270.3 2.6 copy-start.1
  276.3 1.7 copy-start.41
  278.6 1.5 copy-start.37
  278.6 1.9 copy-start.38
  281.3 1.5 copy-start.28
  281.5 1.7 copy-start.26
  281.5 2.1 copy-start.27
  284.4 1.5 copy-start.34
  284.4 1.9 copy-start.35
  288.0 1.7 copy-start.33
  294.4 1.3 copy-start.56
  303.3 2.0 copy-start.23
  (25 other events, 28.5 us)
where the time goes:
time: 316 us; the launch traced here: 310 us
  matrix products  92.7 us (29%)
  waiting for transfers between devices  87.5 us (28%)
  local copies, waits for them, and re-layouts  46.8 us (15%)
  blocking collectives  34.7 us (11%)
  starting transfers between devices  34.3 us (11%)
  other arithmetic  11.6 us (4%)
    dot_general x163, matrix products, band_product(): jnp.einsum('nxy,nyz->nxz', left[:, a + left_half], rows_b, preferred_elem...  92.7 us
    ppermute x3, waiting for transfers between devices, with_halo(): before = lax.ppermute(last, axis, up)  51.5 us
    ppermute x3, waiting for transfers between devices, with_halo(): after = lax.ppermute(leading, axis, down)  36 us
    all_to_all x1, blocking collectives, shards(): lax.all_to_all(h_send, 'dom', split_axis=0, concat_axis=0, tiled=True)  34.7 us
    unnamed x136, local copies, waits for them, and re-layouts  28.9 us
    ppermute x3, starting transfers between devices, with_halo(): before = lax.ppermute(last, axis, up)  12.4 us
    all_to_all x1, starting transfers between devices, shards(): lax.all_to_all(p_send, 'dom', split_axis=0, concat_axis=0, tiled=True)  8.26 us
    ppermute x3, starting transfers between devices, with_halo(): after = lax.ppermute(leading, axis, down)  7.38 us
  transfers between devices with their start and end apart: 8, of which 4 were waited for; matrix products, arithmetic and copies ran while one was open for 10% of the time, Pallas kernels for 0%

commit v1 on v0

v1 whole, which is shorter than its diff:
```python
import functools

import jax
import jax.numpy as jnp
from jax import lax
from jax.experimental import pallas as pl
from jax.experimental.pallas import tpu as pltpu
from jax.sharding import PartitionSpec as P

MESH = pl.DeviceIdType.MESH
BAND = 5
P_HALO, H_HALO, X_HALO = 6, 4, 4

P_PARTS = ((2, 2, 0, 5), (3, 1, 1, 4), (4, 1, 2, 3), (5, 1, 3, 2), (6, 1, 4, 1))
H_PARTS = ((4, 4, 0, 5),)
X_PARTS = ((1, 1, 1, 4), (2, 1, 2, 3), (3, 1, 3, 2), (4, 1, 4, 1))
PARTS = (P_PARTS, H_PARTS, X_PARTS)
HALOS = (P_HALO, H_HALO, X_HALO)


def kernel(
    domains,
    group,
    side,
    rows,
    home,
    p_mask,
    h_mask,
    x_mask,
    p_hbm,
    h_hbm,
    x_hbm,
    d_hbm,
    e_hbm,
    p_in,
    h_in,
    x_in,
    p_send,
    h_send,
    p_recv,
    h_recv,
    p_win,
    h_win,
    x_win,
    left,
    weighted,
    middle,
    d_out,
    e_out,
    meta_send,
    meta_recv,
    meta,
    local_sem,
    slot_send,
    slot_recv,
    halo_send,
    halo_recv,
    out_sem,
):
    g, t = lax.axis_index("grid"), lax.axis_index("dom")
    tx, tz = t // side, t % side
    block = p_in.shape[-1]
    me = g * group + t
    has_next, has_prev = me < domains * group - 1, me > 0
    after = lax.rem(me + 1, domains * group)
    before = lax.rem(me + domains * group - 1, domains * group)
    next_id = (after // group, after % group)
    prev_id = (before // group, before % group)

    def target(rel):
        return lax.rem(tx + rel // side, side) * side + lax.rem(tz + rel % side, side)

    loads = [
        pltpu.make_async_copy(src, dst, local_sem.at[i])
        for i, (src, dst) in enumerate(((p_hbm, p_in), (x_hbm, x_in), (h_hbm, h_in)))
    ]
    for load in loads:
        load.start()

    barrier = pltpu.get_barrier_semaphore()

    @pl.loop(1, group)
    def _(rel):
        pl.semaphore_signal(barrier, inc=1, device_id=(g, target(rel)), device_id_type=MESH)

    cross_next = (t == group - 1) & has_next
    cross_prev = (t == 0) & has_prev

    @pl.when(cross_next)
    def _():
        pl.semaphore_signal(barrier, inc=1, device_id=next_id, device_id_type=MESH)

    @pl.when(cross_prev)
    def _():
        pl.semaphore_signal(barrier, inc=1, device_id=prev_id, device_id_type=MESH)

    homes = [home[r] for r in range(rows)]
    devs = [(h // rows) % group for h in homes]
    lane = lax.broadcasted_iota(jnp.int32, (8, 128), 1)
    packed = jnp.zeros((8, 128), jnp.int32)
    for r in range(rows):
        packed = jnp.where(lane == r, homes[r], packed)
    meta_send[...] = packed
    meta_recv[0] = packed

    cross = cross_next.astype(jnp.int32) + cross_prev.astype(jnp.int32)
    pl.semaphore_wait(barrier, group - 1 + cross)

    def slot_copy(kind, src, dst, rel):
        return pltpu.make_async_remote_copy(
            src_ref=src,
            dst_ref=dst,
            send_sem=slot_send.at[kind, rel],
            recv_sem=slot_recv.at[kind, rel],
            device_id=(g, target(rel)),
            device_id_type=MESH,
        )

    def meta_copy(rel):
        return slot_copy(2, meta_send, meta_recv.at[rel], rel)

    def p_copy(rel):
        return slot_copy(0, p_send.at[rel], p_recv.at[rel], rel)

    def h_copy(rel):
        return slot_copy(1, h_send.at[rel], h_recv.at[rel], rel)

    def masked(ref, mask, row, b):
        scale = jnp.full((block, block), mask[row, b].astype(jnp.float32)).astype(jnp.bfloat16)
        return ref[row, b] * scale

    def fill(ref, mask, out, slot, rel):
        to = target(rel)
        row = jnp.int32(0)
        for r in range(rows):
            row = jnp.where(devs[r] == to, r, row)
        for b in range(BAND):
            out[slot, b] = masked(ref, mask, row, b)

    @pl.loop(1, group)
    def _(rel):
        meta_copy(rel).start()

    loads[0].wait()

    @pl.loop(1, group)
    def _(rel):
        fill(p_in, p_mask, p_send, rel, rel)
        p_copy(rel).start()

    fill(p_in, p_mask, p_recv, 0, 0)

    windows = (p_win, h_win, x_win)

    def halo_copies(m):
        win, halo = windows[m], HALOS[m]
        up, down = [], []
        for c, (far, n, b0, nb) in enumerate(PARTS[m]):
            low = halo + rows - far
            up.append(
                pltpu.make_async_remote_copy(
                    src_ref=win.at[pl.ds(low, n), pl.ds(b0, nb)],
                    dst_ref=win.at[pl.ds(low - rows, n), pl.ds(b0, nb)],
                    send_sem=halo_send.at[m, 0, c],
                    recv_sem=halo_recv.at[m, 0, c],
                    device_id=next_id,
                    device_id_type=MESH,
                )
            )
            high, b1 = halo + far - n, BAND - b0 - nb
            down.append(
                pltpu.make_async_remote_copy(
                    src_ref=win.at[pl.ds(high, n), pl.ds(b1, nb)],
                    dst_ref=win.at[pl.ds(high + rows, n), pl.ds(b1, nb)],
                    send_sem=halo_send.at[m, 1, c],
                    recv_sem=halo_recv.at[m, 1, c],
                    device_id=prev_id,
                    device_id_type=MESH,
                )
            )
        return up, down

    def start_halo(m):
        up, down = halo_copies(m)

        @pl.when(has_next)
        def _():
            for copy in up:
                copy.start()

        @pl.when(has_prev)
        def _():
            for copy in down:
                copy.start()

    def wait_halo(m):
        up, down = halo_copies(m)

        @pl.when(has_prev)
        def _():
            for copy in up:
                copy.wait_recv()

        @pl.when(has_next)
        def _():
            for copy in down:
                copy.wait_recv()

    def wait_halo_sent(m):
        up, down = halo_copies(m)

        @pl.when(has_next)
        def _():
            for copy in up:
                copy.wait_send()

        @pl.when(has_prev)
        def _():
            for copy in down:
                copy.wait_send()

    def clear(win, first, count):
        @pl.loop(first, first + count)
        def _(row):
            for b in range(BAND):
                win[row, b] = jnp.zeros((block, block), jnp.bfloat16)

    @pl.when(jnp.logical_not(has_prev))
    def _():
        for win, halo in zip(windows, HALOS):
            clear(win, 0, halo)

    @pl.when(jnp.logical_not(has_next))
    def _():
        for win, halo in zip(windows, HALOS):
            clear(win, halo + rows, halo)

    loads[1].wait()

    @pl.loop(0, rows)
    def _(row):
        for b in range(BAND):
            x_win[X_HALO + row, b] = masked(x_in, x_mask, row, b)

    start_halo(2)
    loads[2].wait()

    @pl.loop(1, group)
    def _(rel):
        fill(h_in, h_mask, h_send, rel, rel)
        h_copy(rel).start()

    fill(h_in, h_mask, h_recv, 0, 0)

    @pl.loop(1, group)
    def _(rel):
        meta_copy(rel).wait_recv()

    to_scalar = pltpu.make_async_copy(meta_recv, meta, local_sem.at[3])
    to_scalar.start()
    to_scalar.wait()

    def find(slot, found):
        for r in range(rows):
            value = meta[slot, 0, r]
            found = tuple(
                jnp.where(value == me * rows + j, slot, found[j]) for j in range(rows)
            )
        return found

    slots = lax.fori_loop(0, group, find, tuple(jnp.int32(0) for _ in range(rows)))

    def place(recv, win, halo):
        for j in range(rows):
            for b in range(BAND):
                win[halo + j, b] = recv[slots[j], b]

    @pl.loop(1, group)
    def _(rel):
        p_copy(rel).wait_recv()

    place(p_recv, p_win, P_HALO)
    start_halo(0)

    def piece(ref, halo, i, dr, dc):
        b = dc - dr + BAND // 2
        if 0 <= b < BAND:
            return ref[halo + 2 * i + dr, b]
        return jnp.zeros((block, block), jnp.bfloat16)

    def panel(ref, halo, i, o, low, high):
        return jnp.concatenate(
            [
                jnp.concatenate([piece(ref, halo, i, dr, 2 * o + c) for c in range(2)], 1)
                for dr in range(2 * low, 2 * high + 2)
            ],
            0,
        )

    def product(a, b):
        return jnp.dot(a, b, preferred_element_type=jnp.float32).astype(jnp.bfloat16)

    two = 2 * block

    def store(out, i, o, value):
        for r in range(2):
            for c in range(2):
                b = 2 * o + c - r + BAND // 2
                if 0 <= b < BAND:
                    out[2 * i + r, b] = value[
                        r * block : (r + 1) * block, c * block : (c + 1) * block
                    ]

    wait_halo(2)
    wait_halo(0)

    @pl.loop(0, rows // 2)
    def _(i):
        x_rows = jnp.concatenate(
            [
                jnp.concatenate([piece(x_win, X_HALO, i, r, dc) for dc in range(-2, 4)], 1)
                for r in range(2)
            ],
            0,
        )
        for o in range(-2, 3):
            low, high = max(-1, o - 1), min(1, o + 1)
            left[i, :, (o + 2) * two : (o + 3) * two] = product(
                x_rows[:, (low + 1) * two : (high + 2) * two],
                panel(p_win, P_HALO, i, o, low, high),
            )
        for o in range(-1, 2):
            store(
                d_out,
                i,
                o,
                product(
                    left[i, :, (o + 1) * two : (o + 4) * two],
                    panel(x_win, X_HALO, i, o, o - 1, o + 1),
                ),
            )

    d_copy = pltpu.make_async_copy(d_out, d_hbm, out_sem.at[0])
    d_copy.start()

    @pl.loop(1, group)
    def _(rel):
        h_copy(rel).wait_recv()

    place(h_recv, h_win, H_HALO)
    start_halo(1)
    wait_halo(1)

    @pl.loop(0, rows // 2)
    def _(i):
        for o in range(-3, 4):
            low, high = max(-2, o - 1), min(2, o + 1)
            weighted[:, (o + 3) * two : (o + 4) * two] = product(
                left[i, :, (low + 2) * two : (high + 3) * two],
                panel(h_win, H_HALO, i, o, low, high),
            )
        for o in range(-2, 3):
            middle[:, (o + 2) * two : (o + 3) * two] = product(
                weighted[:, (o + 2) * two : (o + 5) * two],
                panel(p_win, P_HALO, i, o, o - 1, o + 1),
            )
        for o in range(-1, 2):
            store(
                e_out,
                i,
                o,
                product(
                    middle[:, (o + 1) * two : (o + 4) * two],
                    panel(x_win, X_HALO, i, o, o - 1, o + 1),
                ),
            )

    e_copy = pltpu.make_async_copy(e_out, e_hbm, out_sem.at[1])
    e_copy.start()

    @pl.loop(1, group)
    def _(rel):
        meta_copy(rel).wait_send()
        p_copy(rel).wait_send()
        h_copy(rel).wait_send()

    for m in range(3):
        wait_halo_sent(m)
    d_copy.wait()
    e_copy.wait()


def solution(mesh):
    domains, group = mesh.shape["grid"], mesh.shape["dom"]
    side = 4

    def shards(home, p_grid, p_mask, h_grid, h_mask, x_inv, x_mask):
        rows, band, block, _ = p_grid.shape
        kind = p_grid.dtype
        two = 2 * block
        own = (rows, band, block, block)
        slots = (group, band, block, block)
        out = jax.ShapeDtypeStruct(own, kind)
        smem = pl.BlockSpec(memory_space=pltpu.SMEM)
        anywhere = pl.BlockSpec(memory_space=pl.ANY)
        return pl.pallas_call(
            functools.partial(kernel, domains, group, side, rows),
            out_shape=(out, out),
            in_specs=[smem] * 4 + [anywhere] * 3,
            out_specs=(anywhere, anywhere),
            scratch_shapes=[
                pltpu.VMEM(own, kind),
                pltpu.VMEM(own, kind),
                pltpu.VMEM(own, kind),
                pltpu.VMEM(slots, kind),
                pltpu.VMEM(slots, kind),
                pltpu.VMEM(slots, kind),
                pltpu.VMEM(slots, kind),
                pltpu.VMEM((rows + 2 * P_HALO, band, block, block), kind),
                pltpu.VMEM((rows + 2 * H_HALO, band, block, block), kind),
                pltpu.VMEM((rows + 2 * X_HALO, band, block, block), kind),
                pltpu.VMEM((rows // 2, two, 5 * two), kind),
                pltpu.VMEM((two, 7 * two), kind),
                pltpu.VMEM((two, 5 * two), kind),
                pltpu.VMEM(own, kind),
                pltpu.VMEM(own, kind),
                pltpu.VMEM((8, 128), jnp.int32),
                pltpu.VMEM((group, 8, 128), jnp.int32),
                pltpu.SMEM((group, 8, 128), jnp.int32),
                pltpu.SemaphoreType.DMA((4,)),
                pltpu.SemaphoreType.DMA((3, group)),
                pltpu.SemaphoreType.DMA((3, group)),
                pltpu.SemaphoreType.DMA((3, 2, 5)),
                pltpu.SemaphoreType.DMA((3, 2, 5)),
                pltpu.SemaphoreType.DMA((2,)),
            ],
            compiler_params=pltpu.CompilerParams(
                collective_id=0, has_side_effects=True, vmem_limit_bytes=48 << 20
            ),
        )(home, p_mask, h_mask, x_mask, p_grid, h_grid, x_inv)

    rows_spec = P(("grid", "dom"))
    return jax.shard_map(
        shards,
        mesh=mesh,
        in_specs=(rows_spec,) * 7,
        out_specs=(rows_spec, rows_spec),
        check_vma=False,
    )
```

time: 316 us -> 143 us (0.45)
  the two profiles are of different devices: /device:TPU:119 before, /device:TPU:26 now
where the time goes in v1:
time: 143 us
  Pallas kernels  135 us (94%)
  local copies, waits for them, and re-layouts  7.45 us (5%)
    pallas_call x1, Pallas kernels, shards(): pl.pallas_call(functools.partial(kernel, domains, group, side, rows), out...  135 us
    unnamed x14, local copies, waits for them, and re-layouts  7.45 us

profile of v1, /device:TPU:26, one launch (start us, length us, event | category | flops | bytes accessed | tf_op | source)
XLA Modules:
  0.0 142.8 jit_solution(16388571824936006471)
XLA Ops:
  0.6 0.0 copy-start
  0.6 1.3 copy-done
  1.9 0.0 copy-start.1
  2.0 1.3 copy-done.1
  3.3 0.0 copy-start.2
  3.3 0.7 copy-done.2
  4.0 0.0 copy-start.3
  4.0 0.7 copy-done.3
  4.6 0.0 copy-start.4
  4.6 0.7 copy-done.4
  5.3 0.0 copy-start.5
  5.3 0.7 copy-done.5
  6.0 134.7 %shard_map.86 = (bf16[8,5,128,128]{3,2,1,0:T(8,128)(2,1)S(1)}, bf16[8,5,128,128]{3,2,1,0:T(8,128)(2,1)S(1)}) custom-call(s32[8]{0:T(128)S(1)} %copy-done.5, s32[8,5]{1,0:T(8,128)S(1)} %copy-done.2, s32[8,5]{1,0:T(8,128)S(1)} %copy-done.3, s32[8,5]{1,0:T(8,128)S(1)} %copy-done.4, bf16[8,5,128,128]{3,2,1,0:T(8,128)(2,1)S(1)} %copy-done, ...), custom_call_target="tpu_custom_call" | custom-call | tf_op jit(solution)/shard_map/pallas_call | solution.py:406
  140.7 1.1 copy.11
  141.7 1.1 copy.12
Async XLA Ops:
  0.6 1.3 copy-start
  1.9 1.3 copy-start.1
  3.3 0.7 copy-start.2
  4.0 0.7 copy-start.3
  4.6 0.7 copy-start.4
  5.3 0.7 copy-start.5

commit v2 on v1

--- a/solution.py
+++ b/solution.py
@@ -14,6 +14,10 @@
 P_PARTS = ((2, 2, 0, 5), (3, 1, 1, 4), (4, 1, 2, 3), (5, 1, 3, 2), (6, 1, 4, 1))
 H_PARTS = ((4, 4, 0, 5),)
 X_PARTS = ((1, 1, 1, 4), (2, 1, 2, 3), (3, 1, 3, 2), (4, 1, 4, 1))
+ORDER = (
+    (1, 0), (0, 1), (3, 0), (0, 3), (2, 0), (0, 2), (1, 1), (3, 3),
+    (1, 3), (3, 1), (2, 1), (2, 3), (1, 2), (3, 2), (2, 2),
+)
 PARTS = (P_PARTS, H_PARTS, X_PARTS)
 HALOS = (P_HALO, H_HALO, X_HALO)
 
@@ -23,10 +27,10 @@
     group,
     side,
     rows,
-    home,
-    p_mask,
-    h_mask,
-    x_mask,
+    home_hbm,
+    p_mask_hbm,
+    h_mask_hbm,
+    x_mask_hbm,
     p_hbm,
     h_hbm,
     x_hbm,
@@ -50,6 +54,10 @@
     meta_send,
     meta_recv,
     meta,
+    home,
+    p_mask,
+    h_mask,
+    x_mask,
     local_sem,
     slot_send,
     slot_recv,
@@ -72,7 +80,17 @@
 
     loads = [
         pltpu.make_async_copy(src, dst, local_sem.at[i])
-        for i, (src, dst) in enumerate(((p_hbm, p_in), (x_hbm, x_in), (h_hbm, h_in)))
+        for i, (src, dst) in enumerate(
+            (
+                (home_hbm, home),
+                (p_mask_hbm, p_mask),
+                (p_hbm, p_in),
+                (x_mask_hbm, x_mask),
+                (x_hbm, x_in),
+                (h_mask_hbm, h_mask),
+                (h_hbm, h_in),
+            )
+        )
     ]
     for load in loads:
         load.start()
@@ -94,6 +112,7 @@
     def _():
         pl.semaphore_signal(barrier, inc=1, device_id=prev_id, device_id_type=MESH)
 
+    loads[0].wait()
     homes = [home[r] for r in range(rows)]
     devs = [(h // rows) % group for h in homes]
     lane = lax.broadcasted_iota(jnp.int32, (8, 128), 1)
@@ -141,10 +160,10 @@
     def _(rel):
         meta_copy(rel).start()
 
-    loads[0].wait()
-
-    @pl.loop(1, group)
-    def _(rel):
+    order = [dx * side + dz for dx, dz in ORDER]
+    loads[1].wait()
+    loads[2].wait()
+    for rel in order:
         fill(p_in, p_mask, p_send, rel, rel)
         p_copy(rel).start()
 
@@ -235,7 +254,8 @@
         for win, halo in zip(windows, HALOS):
             clear(win, halo + rows, halo)
 
-    loads[1].wait()
+    loads[3].wait()
+    loads[4].wait()
 
     @pl.loop(0, rows)
     def _(row):
@@ -243,10 +263,9 @@
             x_win[X_HALO + row, b] = masked(x_in, x_mask, row, b)
 
     start_halo(2)
-    loads[2].wait()
-
-    @pl.loop(1, group)
-    def _(rel):
+    loads[5].wait()
+    loads[6].wait()
+    for rel in order:
         fill(h_in, h_mask, h_send, rel, rel)
         h_copy(rel).start()
 
@@ -256,7 +275,7 @@
     def _(rel):
         meta_copy(rel).wait_recv()
 
-    to_scalar = pltpu.make_async_copy(meta_recv, meta, local_sem.at[3])
+    to_scalar = pltpu.make_async_copy(meta_recv, meta, local_sem.at[7])
     to_scalar.start()
     to_scalar.wait()
 
@@ -401,12 +420,11 @@
         own = (rows, band, block, block)
         slots = (group, band, block, block)
         out = jax.ShapeDtypeStruct(own, kind)
-        smem = pl.BlockSpec(memory_space=pltpu.SMEM)
         anywhere = pl.BlockSpec(memory_space=pl.ANY)
         return pl.pallas_call(
             functools.partial(kernel, domains, group, side, rows),
             out_shape=(out, out),
-            in_specs=[smem] * 4 + [anywhere] * 3,
+            in_specs=[anywhere] * 7,
             out_specs=(anywhere, anywhere),
             scratch_shapes=[
                 pltpu.VMEM(own, kind),
@@ -427,7 +445,11 @@
                 pltpu.VMEM((8, 128), jnp.int32),
                 pltpu.VMEM((group, 8, 128), jnp.int32),
                 pltpu.SMEM((group, 8, 128), jnp.int32),
-                pltpu.SemaphoreType.DMA((4,)),
+                pltpu.SMEM((rows,), jnp.int32),
+                pltpu.SMEM((rows, band), jnp.int32),
+                pltpu.SMEM((rows, band), jnp.int32),
+                pltpu.SMEM((rows, band), jnp.int32),
+                pltpu.SemaphoreType.DMA((8,)),
                 pltpu.SemaphoreType.DMA((3, group)),
                 pltpu.SemaphoreType.DMA((3, group)),
                 pltpu.SemaphoreType.DMA((3, 2, 5)),
@@ -435,7 +457,7 @@
                 pltpu.SemaphoreType.DMA((2,)),
             ],
             compiler_params=pltpu.CompilerParams(
-                collective_id=0, has_side_effects=True, vmem_limit_bytes=48 << 20
+                collective_id=0, has_side_effects=True, vmem_limit_bytes=60 << 20
             ),
         )(home, p_mask, h_mask, x_mask, p_grid, h_grid, x_inv)
 

time: 143 us -> 131 us (0.916)
  Pallas kernels: 135 us -> 127 us
  local copies, waits for them, and re-layouts: 7.45 us -> 3.69 us
    pallas_call x1, Pallas kernels: 135 us -> 127 us  [shards(): pl.pallas_call(functools.partial(kernel, domains, group, side, rows), out...]
    unnamed x14 -> x4, local copies, waits for them, and re-layouts: 7.45 us -> 3.69 us
where the time goes in v2:
time: 131 us
  Pallas kernels  127 us (97%)
  local copies, waits for them, and re-layouts  3.69 us (3%)
    pallas_call x1, Pallas kernels, shards(): pl.pallas_call(functools.partial(kernel, domains, group, side, rows), out...  127 us
    unnamed x4, local copies, waits for them, and re-layouts  3.69 us

profile of v2, /device:TPU:26, one launch (start us, length us, event | category | flops | bytes accessed | tf_op | source)
XLA Modules:
  0.0 131.2 jit_solution(14092675326735098032)
XLA Ops:
  0.6 126.8 %shard_map.86 = (bf16[8,5,128,128]{3,2,1,0:T(8,128)(2,1)}, bf16[8,5,128,128]{3,2,1,0:T(8,128)(2,1)}) custom-call(s32[8]{0:T(128)} %home_hbm.1, s32[8,5]{1,0:T(8,128)} %p_mask_hbm.1, s32[8,5]{1,0:T(8,128)} %h_mask_hbm.1, s32[8,5]{1,0:T(8,128)} %x_mask_hbm.1, bf16[8,5,128,128]{3,2,1,0:T(8,128)(2,1)} %p_hbm.1, bf16[8,5,128,128]{3,2,1,0:T(8,128)(2,1)} %h_hbm.1, ...), custom_call_target="tpu_custom_call" | custom-call | tf_op jit(solution)/shard_map/pallas_call | solution.py:424
  127.5 0.0 copy-start
  127.5 2.6 %copy.11 = bf16[8,5,128,128]{3,2,1,0:T(8,128)(2,1)} copy(bf16[8,5,128,128]{3,2,1,0:T(8,128)(2,1)} %get-tuple-element.4) | data formatting | bytes 2621440
  130.1 0.0 copy-done
  130.1 1.1 copy.12
Async XLA Ops:
  127.5 2.6 %copy-start = (bf16[8,5,128,128]{3,2,1,0:T(8,128)(2,1)S(1)}, bf16[8,5,128,128]{3,2,1,0:T(8,128)(2,1)}, u32[]{:S(2)}) copy-start(bf16[8,5,128,128]{3,2,1,0:T(8,128)(2,1)} %get-tuple-element.5) | copy-start | bytes 3932164

commit v3 on v2

--- a/solution.py
+++ b/solution.py
@@ -12,7 +12,8 @@
 P_HALO, H_HALO, X_HALO = 6, 4, 4
 
 P_PARTS = ((2, 2, 0, 5), (3, 1, 1, 4), (4, 1, 2, 3), (5, 1, 3, 2), (6, 1, 4, 1))
-H_PARTS = ((4, 4, 0, 5),)
+H_CUTS = ((0, 3), (3, 2))
+H_PARTS = tuple((4, 4, b0, nb) for b0, nb in H_CUTS)
 X_PARTS = ((1, 1, 1, 4), (2, 1, 2, 3), (3, 1, 3, 2), (4, 1, 4, 1))
 ORDER = (
     (1, 0), (0, 1), (3, 0), (0, 3), (2, 0), (0, 2), (1, 1), (3, 3),
@@ -42,13 +43,13 @@
     p_send,
     h_send,
     p_recv,
-    h_recv,
+    h_recv_0,
+    h_recv_1,
     p_win,
     h_win,
     x_win,
-    left,
+    factors,
     weighted,
-    middle,
     d_out,
     e_out,
     meta_send,
@@ -122,9 +123,6 @@
     meta_send[...] = packed
     meta_recv[0] = packed
 
-    cross = cross_next.astype(jnp.int32) + cross_prev.astype(jnp.int32)
-    pl.semaphore_wait(barrier, group - 1 + cross)
-
     def slot_copy(kind, src, dst, rel):
         return pltpu.make_async_remote_copy(
             src_ref=src,
@@ -141,30 +139,38 @@
     def p_copy(rel):
         return slot_copy(0, p_send.at[rel], p_recv.at[rel], rel)
 
-    def h_copy(rel):
-        return slot_copy(1, h_send.at[rel], h_recv.at[rel], rel)
+    h_recv = (h_recv_0, h_recv_1)
+
+    def h_copy(rel, part):
+        cut = pl.ds(*H_CUTS[part])
+        return slot_copy((1, 3)[part], h_send.at[rel, cut], h_recv[part].at[rel], rel)
 
     def masked(ref, mask, row, b):
         scale = jnp.full((block, block), mask[row, b].astype(jnp.float32)).astype(jnp.bfloat16)
         return ref[row, b] * scale
 
-    def fill(ref, mask, out, slot, rel):
+    def fill(ref, mask, out, slot, rel, first=0, count=BAND):
         to = target(rel)
         row = jnp.int32(0)
         for r in range(rows):
             row = jnp.where(devs[r] == to, r, row)
-        for b in range(BAND):
-            out[slot, b] = masked(ref, mask, row, b)
-
-    @pl.loop(1, group)
-    def _(rel):
-        meta_copy(rel).start()
+        for b in range(count):
+            out[slot, b] = masked(ref, mask, row, first + b)
 
     order = [dx * side + dz for dx, dz in ORDER]
     loads[1].wait()
     loads[2].wait()
     for rel in order:
         fill(p_in, p_mask, p_send, rel, rel)
+
+    cross = cross_next.astype(jnp.int32) + cross_prev.astype(jnp.int32)
+    pl.semaphore_wait(barrier, group - 1 + cross)
+
+    @pl.loop(1, group)
+    def _(rel):
+        meta_copy(rel).start()
+
+    for rel in order:
         p_copy(rel).start()
 
     fill(p_in, p_mask, p_recv, 0, 0)
@@ -186,7 +192,7 @@
                     device_id_type=MESH,
                 )
             )
-            high, b1 = halo + far - n, BAND - b0 - nb
+            high, b1 = halo + far - n, b0 if m == 1 else BAND - b0 - nb
             down.append(
                 pltpu.make_async_remote_copy(
                     src_ref=win.at[pl.ds(high, n), pl.ds(b1, nb)],
@@ -199,18 +205,11 @@
             )
         return up, down
 
-    def start_halo(m):
+    def start_halo(m, parts=None):
         up, down = halo_copies(m)
-
-        @pl.when(has_next)
-        def _():
-            for copy in up:
-                copy.start()
-
-        @pl.when(has_prev)
-        def _():
-            for copy in down:
-                copy.start()
+        for c in range(len(up)) if parts is None else parts:
+            pl.when(has_next)(up[c].start)
+            pl.when(has_prev)(down[c].start)
 
     def wait_halo(m):
         up, down = halo_copies(m)
@@ -244,6 +243,25 @@
             for b in range(BAND):
                 win[row, b] = jnp.zeros((block, block), jnp.bfloat16)
 
+    loads[3].wait()
+    loads[4].wait()
+
+    @pl.loop(0, rows)
+    def _(row):
+        for b in range(BAND):
+            x_win[X_HALO + row, b] = masked(x_in, x_mask, row, b)
+
+    loads[5].wait()
+    loads[6].wait()
+    for rel in order:
+        fill(h_in, h_mask, h_send, rel, rel)
+        h_copy(rel, 0).start()
+    for rel in order:
+        h_copy(rel, 1).start()
+
+    for recv, cut in zip(h_recv, H_CUTS):
+        fill(h_in, h_mask, recv, 0, 0, *cut)
+
     @pl.when(jnp.logical_not(has_prev))
     def _():
         for win, halo in zip(windows, HALOS):
@@ -254,28 +272,11 @@
         for win, halo in zip(windows, HALOS):
             clear(win, halo + rows, halo)
 
-    loads[3].wait()
-    loads[4].wait()
-
-    @pl.loop(0, rows)
-    def _(row):
-        for b in range(BAND):
-            x_win[X_HALO + row, b] = masked(x_in, x_mask, row, b)
-
-    start_halo(2)
-    loads[5].wait()
-    loads[6].wait()
-    for rel in order:
-        fill(h_in, h_mask, h_send, rel, rel)
-        h_copy(rel).start()
-
-    fill(h_in, h_mask, h_recv, 0, 0)
-
     @pl.loop(1, group)
     def _(rel):
         meta_copy(rel).wait_recv()
 
-    to_scalar = pltpu.make_async_copy(meta_recv, meta, local_sem.at[7])
+    to_scalar = pltpu.make_async_copy(meta_recv.at[:, pl.ds(0, 1)], meta, local_sem.at[7])
     to_scalar.start()
     to_scalar.wait()
 
@@ -289,10 +290,10 @@
 
     slots = lax.fori_loop(0, group, find, tuple(jnp.int32(0) for _ in range(rows)))
 
-    def place(recv, win, halo):
+    def place(recv, win, halo, first=0, count=BAND):
         for j in range(rows):
-            for b in range(BAND):
-                win[halo + j, b] = recv[slots[j], b]
+            for b in range(count):
+                win[halo + j, first + b] = recv[slots[j], b]
 
     @pl.loop(1, group)
     def _(rel):
@@ -330,7 +331,16 @@
                         r * block : (r + 1) * block, c * block : (c + 1) * block
                     ]
 
-    wait_halo(2)
+    for part, cut in enumerate(H_CUTS):
+
+        @pl.loop(1, group)
+        def _(rel):
+            h_copy(rel, part).wait_recv()
+
+        place(h_recv[part], h_win, H_HALO, *cut)
+        start_halo(1, (part,))
+
+    start_halo(2)
     wait_halo(0)
 
     @pl.loop(0, rows // 2)
@@ -344,30 +354,11 @@
         )
         for o in range(-2, 3):
             low, high = max(-1, o - 1), min(1, o + 1)
-            left[i, :, (o + 2) * two : (o + 3) * two] = product(
+            factors[i, pl.ds(0, two), (o + 2) * two : (o + 3) * two] = product(
                 x_rows[:, (low + 1) * two : (high + 2) * two],
                 panel(p_win, P_HALO, i, o, low, high),
             )
-        for o in range(-1, 2):
-            store(
-                d_out,
-                i,
-                o,
-                product(
-                    left[i, :, (o + 1) * two : (o + 4) * two],
-                    panel(x_win, X_HALO, i, o, o - 1, o + 1),
-                ),
-            )
-
-    d_copy = pltpu.make_async_copy(d_out, d_hbm, out_sem.at[0])
-    d_copy.start()
-
-    @pl.loop(1, group)
-    def _(rel):
-        h_copy(rel).wait_recv()
-
-    place(h_recv, h_win, H_HALO)
-    start_halo(1)
+
     wait_halo(1)
 
     @pl.loop(0, rows // 2)
@@ -375,25 +366,29 @@
         for o in range(-3, 4):
             low, high = max(-2, o - 1), min(2, o + 1)
             weighted[:, (o + 3) * two : (o + 4) * two] = product(
-                left[i, :, (low + 2) * two : (high + 3) * two],
+                factors[i, pl.ds(0, two), (low + 2) * two : (high + 3) * two],
                 panel(h_win, H_HALO, i, o, low, high),
             )
         for o in range(-2, 3):
-            middle[:, (o + 2) * two : (o + 3) * two] = product(
+            factors[i, pl.ds(two, two), (o + 2) * two : (o + 3) * two] = product(
                 weighted[:, (o + 2) * two : (o + 5) * two],
                 panel(p_win, P_HALO, i, o, o - 1, o + 1),
             )
+
+    wait_halo(2)
+
+    @pl.loop(0, rows // 2)
+    def _(i):
         for o in range(-1, 2):
-            store(
-                e_out,
-                i,
-                o,
-                product(
-                    middle[:, (o + 1) * two : (o + 4) * two],
-                    panel(x_win, X_HALO, i, o, o - 1, o + 1),
-                ),
-            )
-
+            both = product(
+                factors[i, :, (o + 1) * two : (o + 4) * two],
+                panel(x_win, X_HALO, i, o, o - 1, o + 1),
+            )
+            store(d_out, i, o, both[:two])
+            store(e_out, i, o, both[two:])
+
+    d_copy = pltpu.make_async_copy(d_out, d_hbm, out_sem.at[0])
+    d_copy.start()
     e_copy = pltpu.make_async_copy(e_out, e_hbm, out_sem.at[1])
     e_copy.start()
 
@@ -401,7 +396,8 @@
     def _(rel):
         meta_copy(rel).wait_send()
         p_copy(rel).wait_send()
-        h_copy(rel).wait_send()
+        h_copy(rel, 0).wait_send()
+        h_copy(rel, 1).wait_send()
 
     for m in range(3):
         wait_halo_sent(m)
@@ -433,25 +429,25 @@
                 pltpu.VMEM(slots, kind),
                 pltpu.VMEM(slots, kind),
                 pltpu.VMEM(slots, kind),
-                pltpu.VMEM(slots, kind),
+                pltpu.VMEM((group, H_CUTS[0][1], block, block), kind),
+                pltpu.VMEM((group, H_CUTS[1][1], block, block), kind),
                 pltpu.VMEM((rows + 2 * P_HALO, band, block, block), kind),
                 pltpu.VMEM((rows + 2 * H_HALO, band, block, block), kind),
                 pltpu.VMEM((rows + 2 * X_HALO, band, block, block), kind),
-                pltpu.VMEM((rows // 2, two, 5 * two), kind),
+                pltpu.VMEM((rows // 2, 2 * two, 5 * two), kind),
                 pltpu.VMEM((two, 7 * two), kind),
-                pltpu.VMEM((two, 5 * two), kind),
                 pltpu.VMEM(own, kind),
                 pltpu.VMEM(own, kind),
                 pltpu.VMEM((8, 128), jnp.int32),
                 pltpu.VMEM((group, 8, 128), jnp.int32),
-                pltpu.SMEM((group, 8, 128), jnp.int32),
+                pltpu.SMEM((group, 1, 128), jnp.int32),
                 pltpu.SMEM((rows,), jnp.int32),
                 pltpu.SMEM((rows, band), jnp.int32),
                 pltpu.SMEM((rows, band), jnp.int32),
                 pltpu.SMEM((rows, band), jnp.int32),
                 pltpu.SemaphoreType.DMA((8,)),
-                pltpu.SemaphoreType.DMA((3, group)),
-                pltpu.SemaphoreType.DMA((3, group)),
+                pltpu.SemaphoreType.DMA((4, group)),
+                pltpu.SemaphoreType.DMA((4, group)),
                 pltpu.SemaphoreType.DMA((3, 2, 5)),
                 pltpu.SemaphoreType.DMA((3, 2, 5)),
                 pltpu.SemaphoreType.DMA((2,)),

time: 131 us -> 115 us (0.88); the launches traced: 131 us -> 113 us
  Pallas kernels: 127 us -> 109 us
    pallas_call x1, Pallas kernels: 127 us -> 109 us  [shards(): pl.pallas_call(functools.partial(kernel, domains, group, side, rows), out...]
where the time goes in v3:
time: 115 us; the launch traced here: 113 us
  Pallas kernels  109 us (95%)
  local copies, waits for them, and re-layouts  3.69 us (3%)
    pallas_call x1, Pallas kernels, shards(): pl.pallas_call(functools.partial(kernel, domains, group, side, rows), out...  109 us
    unnamed x4, local copies, waits for them, and re-layouts  3.69 us

profile of v3, /device:TPU:26, one launch (start us, length us, event | category | flops | bytes accessed | tf_op | source)
XLA Modules:
  0.0 112.9 jit_solution(2992025681096157404)
XLA Ops:
  0.6 108.5 %shard_map.86 = (bf16[8,5,128,128]{3,2,1,0:T(8,128)(2,1)}, bf16[8,5,128,128]{3,2,1,0:T(8,128)(2,1)}) custom-call(s32[8]{0:T(128)} %home_hbm.1, s32[8,5]{1,0:T(8,128)} %p_mask_hbm.1, s32[8,5]{1,0:T(8,128)} %h_mask_hbm.1, s32[8,5]{1,0:T(8,128)} %x_mask_hbm.1, bf16[8,5,128,128]{3,2,1,0:T(8,128)(2,1)} %p_hbm.1, bf16[8,5,128,128]{3,2,1,0:T(8,128)(2,1)} %h_hbm.1, ...), custom_call_target="tpu_custom_call" | custom-call | tf_op jit(solution)/shard_map/pallas_call | solution.py:420
  109.2 0.0 copy-start
  109.2 2.6 %copy.11 = bf16[8,5,128,128]{3,2,1,0:T(8,128)(2,1)} copy(bf16[8,5,128,128]{3,2,1,0:T(8,128)(2,1)} %get-tuple-element.4) | data formatting | bytes 2621440
  111.8 0.0 copy-done
  111.8 1.1 copy.12
Async XLA Ops:
  109.2 2.6 %copy-start = (bf16[8,5,128,128]{3,2,1,0:T(8,128)(2,1)S(1)}, bf16[8,5,128,128]{3,2,1,0:T(8,128)(2,1)}, u32[]{:S(2)}) copy-start(bf16[8,5,128,128]{3,2,1,0:T(8,128)(2,1)} %get-tuple-element.5) | copy-start | bytes 3932164

commit v4 on v3

--- a/solution.py
+++ b/solution.py
@@ -35,8 +35,8 @@
     p_hbm,
     h_hbm,
     x_hbm,
-    d_hbm,
-    e_hbm,
+    d_out,
+    e_out,
     p_in,
     h_in,
     x_in,
@@ -50,8 +50,6 @@
     x_win,
     factors,
     weighted,
-    d_out,
-    e_out,
     meta_send,
     meta_recv,
     meta,
@@ -64,7 +62,6 @@
     slot_recv,
     halo_send,
     halo_recv,
-    out_sem,
 ):
     g, t = lax.axis_index("grid"), lax.axis_index("dom")
     tx, tz = t // side, t % side
@@ -375,22 +372,23 @@
                 panel(p_win, P_HALO, i, o, o - 1, o + 1),
             )
 
+    def with_x(i, o):
+        both = product(
+            factors[i, :, (o + 1) * two : (o + 4) * two],
+            panel(x_win, X_HALO, i, o, o - 1, o + 1),
+        )
+        store(d_out, i, o, both[:two])
+        store(e_out, i, o, both[two:])
+
+    pairs = [(i, o) for i in range(rows // 2) for o in range(-1, 2)]
+    inner = [(i, o) for i, o in pairs if 0 < i + o < rows // 2 - 1]
+    for i, o in inner:
+        with_x(i, o)
     wait_halo(2)
-
-    @pl.loop(0, rows // 2)
-    def _(i):
-        for o in range(-1, 2):
-            both = product(
-                factors[i, :, (o + 1) * two : (o + 4) * two],
-                panel(x_win, X_HALO, i, o, o - 1, o + 1),
-            )
-            store(d_out, i, o, both[:two])
-            store(e_out, i, o, both[two:])
-
-    d_copy = pltpu.make_async_copy(d_out, d_hbm, out_sem.at[0])
-    d_copy.start()
-    e_copy = pltpu.make_async_copy(e_out, e_hbm, out_sem.at[1])
-    e_copy.start()
+    for i, o in pairs:
+        if (i, o) not in inner:
+            with_x(i, o)
+
 
     @pl.loop(1, group)
     def _(rel):
@@ -401,8 +399,6 @@
 
     for m in range(3):
         wait_halo_sent(m)
-    d_copy.wait()
-    e_copy.wait()
 
 
 def solution(mesh):
@@ -421,7 +417,7 @@
             functools.partial(kernel, domains, group, side, rows),
             out_shape=(out, out),
             in_specs=[anywhere] * 7,
-            out_specs=(anywhere, anywhere),
+            out_specs=(pl.BlockSpec(memory_space=pltpu.VMEM),) * 2,
             scratch_shapes=[
                 pltpu.VMEM(own, kind),
                 pltpu.VMEM(own, kind),
@@ -436,8 +432,6 @@
                 pltpu.VMEM((rows + 2 * X_HALO, band, block, block), kind),
                 pltpu.VMEM((rows // 2, 2 * two, 5 * two), kind),
                 pltpu.VMEM((two, 7 * two), kind),
-                pltpu.VMEM(own, kind),
-                pltpu.VMEM(own, kind),
                 pltpu.VMEM((8, 128), jnp.int32),
                 pltpu.VMEM((group, 8, 128), jnp.int32),
                 pltpu.SMEM((group, 1, 128), jnp.int32),
@@ -450,12 +444,11 @@
                 pltpu.SemaphoreType.DMA((4, group)),
                 pltpu.SemaphoreType.DMA((3, 2, 5)),
                 pltpu.SemaphoreType.DMA((3, 2, 5)),
-                pltpu.SemaphoreType.DMA((2,)),
             ],
             compiler_params=pltpu.CompilerParams(
-                collective_id=0, has_side_effects=True, vmem_limit_bytes=60 << 20
+                collective_id=0, has_side_effects=True, vmem_limit_bytes=51 << 20
             ),
-        )(home, p_mask, h_mask, x_mask, p_grid, h_grid, x_inv)
+        )(*(pltpu.with_memory_space_constraint(a, pltpu.HBM) for a in (home, p_mask, h_mask, x_mask, p_grid, h_grid, x_inv)))
 
     rows_spec = P(("grid", "dom"))
     return jax.shard_map(

time: 115 us -> 111 us (0.965)
  the two profiles are of different devices: /device:TPU:26 before, /device:TPU:24 now
where the time goes in v4:
time: 111 us
  Pallas kernels  108 us (97%)
  local copies, waits for them, and re-layouts  2.11 us (2%)
    pallas_call x1, Pallas kernels, shards(): pl.pallas_call(functools.partial(kernel, domains, group, side, rows), out...  108 us

profile of v4, /device:TPU:24, one launch (start us, length us, event | category | flops | bytes accessed | tf_op | source)
XLA Modules:
  0.0 110.8 jit_solution(14842714063633868011)
XLA Ops:
  0.6 108.0 %shard_map.86 = (bf16[8,5,128,128]{3,2,1,0:T(8,128)(2,1)S(1)}, bf16[8,5,128,128]{3,2,1,0:T(8,128)(2,1)S(1)}) custom-call(s32[8]{0:T(128)} %home_hbm.1, s32[8,5]{1,0:T(8,128)} %p_mask_hbm.1, s32[8,5]{1,0:T(8,128)} %h_mask_hbm.1, s32[8,5]{1,0:T(8,128)} %x_mask_hbm.1, bf16[8,5,128,128]{3,2,1,0:T(8,128)(2,1)} %p_hbm.1, bf16[8,5,128,128]{3,2,1,0:T(8,128)(2,1)} %h_hbm.1, ...), custom_call_target="tpu_custom_call" | custom-call | tf_op jit(solution)/shard_map/pallas_call | solution.py:416
  108.6 1.1 copy.11
  109.7 1.1 copy.12

commit v5 on v4

--- a/solution.py
+++ b/solution.py
@@ -12,12 +12,12 @@
 P_HALO, H_HALO, X_HALO = 6, 4, 4
 
 P_PARTS = ((2, 2, 0, 5), (3, 1, 1, 4), (4, 1, 2, 3), (5, 1, 3, 2), (6, 1, 4, 1))
-H_CUTS = ((0, 3), (3, 2))
+H_CUTS = ((0, 5),)
 H_PARTS = tuple((4, 4, b0, nb) for b0, nb in H_CUTS)
 X_PARTS = ((1, 1, 1, 4), (2, 1, 2, 3), (3, 1, 3, 2), (4, 1, 4, 1))
 ORDER = (
-    (1, 0), (0, 1), (3, 0), (0, 3), (2, 0), (0, 2), (1, 1), (3, 3),
-    (1, 3), (3, 1), (2, 1), (2, 3), (1, 2), (3, 2), (2, 2),
+    (2, 2), (1, 2), (3, 0), (2, 1), (0, 3), (1, 1), (3, 3), (2, 0),
+    (0, 2), (3, 2), (1, 0), (2, 3), (0, 1), (1, 3), (3, 1),
 )
 PARTS = (P_PARTS, H_PARTS, X_PARTS)
 HALOS = (P_HALO, H_HALO, X_HALO)
@@ -44,7 +44,6 @@
     h_send,
     p_recv,
     h_recv_0,
-    h_recv_1,
     p_win,
     h_win,
     x_win,
@@ -95,9 +94,10 @@
 
     barrier = pltpu.get_barrier_semaphore()
 
-    @pl.loop(1, group)
-    def _(rel):
-        pl.semaphore_signal(barrier, inc=1, device_id=(g, target(rel)), device_id_type=MESH)
+    for dx, dz in ORDER:
+        pl.semaphore_signal(
+            barrier, inc=1, device_id=(g, target(dx * side + dz)), device_id_type=MESH
+        )
 
     cross_next = (t == group - 1) & has_next
     cross_prev = (t == 0) & has_prev
@@ -136,7 +136,7 @@
     def p_copy(rel):
         return slot_copy(0, p_send.at[rel], p_recv.at[rel], rel)
 
-    h_recv = (h_recv_0, h_recv_1)
+    h_recv = (h_recv_0,)
 
     def h_copy(rel, part):
         cut = pl.ds(*H_CUTS[part])
@@ -253,8 +253,6 @@
     for rel in order:
         fill(h_in, h_mask, h_send, rel, rel)
         h_copy(rel, 0).start()
-    for rel in order:
-        h_copy(rel, 1).start()
 
     for recv, cut in zip(h_recv, H_CUTS):
         fill(h_in, h_mask, recv, 0, 0, *cut)
@@ -395,7 +393,6 @@
         meta_copy(rel).wait_send()
         p_copy(rel).wait_send()
         h_copy(rel, 0).wait_send()
-        h_copy(rel, 1).wait_send()
 
     for m in range(3):
         wait_halo_sent(m)
@@ -426,7 +423,6 @@
                 pltpu.VMEM(slots, kind),
                 pltpu.VMEM(slots, kind),
                 pltpu.VMEM((group, H_CUTS[0][1], block, block), kind),
-                pltpu.VMEM((group, H_CUTS[1][1], block, block), kind),
                 pltpu.VMEM((rows + 2 * P_HALO, band, block, block), kind),
                 pltpu.VMEM((rows + 2 * H_HALO, band, block, block), kind),
                 pltpu.VMEM((rows + 2 * X_HALO, band, block, block), kind),

time: 111 us -> 110 us (level)
  the two profiles are of different devices: /device:TPU:24 before, /device:TPU:26 now
where the time goes in v5:
time: 110 us; the launch traced here: 108 us
  Pallas kernels  105 us (95%)
  local copies, waits for them, and re-layouts  2.11 us (2%)
    pallas_call x1, Pallas kernels, shards(): pl.pallas_call(functools.partial(kernel, domains, group, side, rows), out...  105 us

profile of v5, /device:TPU:26, one launch (start us, length us, event | category | flops | bytes accessed | tf_op | source)
XLA Modules:
  0.0 107.6 jit_solution(9754151735053517424)
XLA Ops:
  0.6 104.9 %shard_map.86 = (bf16[8,5,128,128]{3,2,1,0:T(8,128)(2,1)S(1)}, bf16[8,5,128,128]{3,2,1,0:T(8,128)(2,1)S(1)}) custom-call(s32[8]{0:T(128)} %home_hbm.1, s32[8,5]{1,0:T(8,128)} %p_mask_hbm.1, s32[8,5]{1,0:T(8,128)} %h_mask_hbm.1, s32[8,5]{1,0:T(8,128)} %x_mask_hbm.1, bf16[8,5,128,128]{3,2,1,0:T(8,128)(2,1)} %p_hbm.1, bf16[8,5,128,128]{3,2,1,0:T(8,128)(2,1)} %h_hbm.1, ...), custom_call_target="tpu_custom_call" | custom-call | tf_op jit(solution)/shard_map/pallas_call | solution.py:413
  105.5 1.1 copy.11
  106.6 1.1 copy.12

commit v6 on v5

--- a/solution.py
+++ b/solution.py
@@ -15,9 +15,7 @@
 H_CUTS = ((0, 5),)
 H_PARTS = tuple((4, 4, b0, nb) for b0, nb in H_CUTS)
 X_PARTS = ((1, 1, 1, 4), (2, 1, 2, 3), (3, 1, 3, 2), (4, 1, 4, 1))
-ORDER = (
-    (2, 2), (1, 2), (3, 0), (2, 1), (0, 3), (1, 1), (3, 3), (2, 0),
-    (0, 2), (3, 2), (1, 0), (2, 3), (0, 1), (1, 3), (3, 1),
+ORDER = ((2, 2), (1, 2), (3, 0), (2, 1), (0, 3), (3, 2), (1, 0), (2, 3), (0, 1), (2, 0), (0, 2), (1, 1), (3, 3), (1, 3), (3, 1),
 )
 PARTS = (P_PARTS, H_PARTS, X_PARTS)
 HALOS = (P_HALO, H_HALO, X_HALO)
@@ -382,20 +380,21 @@
     inner = [(i, o) for i, o in pairs if 0 < i + o < rows // 2 - 1]
     for i, o in inner:
         with_x(i, o)
-    wait_halo(2)
-    for i, o in pairs:
-        if (i, o) not in inner:
-            with_x(i, o)
-
-
     @pl.loop(1, group)
     def _(rel):
         meta_copy(rel).wait_send()
         p_copy(rel).wait_send()
         h_copy(rel, 0).wait_send()
 
-    for m in range(3):
-        wait_halo_sent(m)
+    wait_halo_sent(0)
+    wait_halo_sent(1)
+    wait_halo(2)
+    for i, o in pairs:
+        if (i, o) not in inner:
+            with_x(i, o)
+
+
+    wait_halo_sent(2)
 
 
 def solution(mesh):

time: 110 us -> 109 us (level)
  no operation moved by 1% of the time
where the time goes in v6:
time: 109 us; the launch traced here: 107 us
  Pallas kernels  105 us (96%)
  local copies, waits for them, and re-layouts  2.11 us (2%)
    pallas_call x1, Pallas kernels, shards(): pl.pallas_call(functools.partial(kernel, domains, group, side, rows), out...  105 us

profile of v6, /device:TPU:26, one launch (start us, length us, event | category | flops | bytes accessed | tf_op | source)
XLA Modules:
  0.0 107.5 jit_solution(1420787167573951793)
XLA Ops:
  0.6 104.7 %shard_map.86 = (bf16[8,5,128,128]{3,2,1,0:T(8,128)(2,1)S(1)}, bf16[8,5,128,128]{3,2,1,0:T(8,128)(2,1)S(1)}) custom-call(s32[8]{0:T(128)} %home_hbm.1, s32[8,5]{1,0:T(8,128)} %p_mask_hbm.1, s32[8,5]{1,0:T(8,128)} %h_mask_hbm.1, s32[8,5]{1,0:T(8,128)} %x_mask_hbm.1, bf16[8,5,128,128]{3,2,1,0:T(8,128)(2,1)} %p_hbm.1, bf16[8,5,128,128]{3,2,1,0:T(8,128)(2,1)} %h_hbm.1, ...), custom_call_target="tpu_custom_call" | custom-call | tf_op jit(solution)/shard_map/pallas_call | solution.py:412
  105.4 1.1 copy.11
  106.4 1.1 copy.12
